TPU v7x, 256 devices: a whole 4x4x8 slice. The times are simulated.
256 devices in a mesh: rep: 4 (over y), blk: 64 (over x, z, core).
Axes of the slice: x: 4, y: 4, z: 8, core: 2. Of those that a mesh axis runs over, the one named last changes fastest.
Arguments:
- feats: bfloat16 [1024, 128, 256], P('blk'), may hold values from -6 to 6
- requests: int32 [64, 64], P('blk'), may hold values from 0 to 15
- tile_dest: int32 [64, 512], P('blk'), may hold values from 0 to 15, as said below
- tile_slot: int32 [64, 512], P('blk'), may hold values from 0 to 63, as said below
- tile_vals: bfloat16 [64, 512, 128, 128], P('blk', None, 'rep'), may hold values from -0.09375 to 0.09375
- w_self: bfloat16 [256, 256], replicated, may hold values from -0.375 to 0.375
- w_neigh: bfloat16 [256, 256], replicated, may hold values from -0.375 to 0.375
- bias: float32 [256], replicated, may hold values from -3 to 3
- cotangent: bfloat16 [1024, 128, 256], P('blk', 'rep'), may hold values from -6 to 6
Outputs:
- hidden: bfloat16 [1024, 128, 256], P('blk', 'rep')
- grad_self: float32 [256, 256], replicated
- grad_neigh: float32 [256, 256], replicated
- grad_bias: float32 [256], replicated
- feat_grad: bfloat16 [1024, 128, 256], P('blk', 'rep')
Inputs may be any that keep to these rules, and one draw needn't show every extreme that they name: `tile_slot`: for each reader b, every owner index is named by exactly 8 of its tiles. `tile_dest`: no two tiles of one reader have both the same destination block and the same owner.
All inputs are finite; a program needn't handle non-finite values.
Results may differ from a plain program's by a relative error of at most 0.015.
Values may be sent and summed in bfloat16 or wider, within the bound.
A program may use at most 128 MiB of HBM per device.

v0:
```python
import math
import jax
import jax.numpy as jnp
from jax import lax
from jax.sharding import PartitionSpec as P


def collect_blocks(arrivals, send_list, blk_dev):
    onehot = (send_list[:, None] == jnp.arange(blk_dev, dtype=jnp.int32)[None, :]).astype(
        jnp.float32
    )
    return jnp.einsum("rb,rjd->bjd", onehot, arrivals, precision=lax.Precision.HIGHEST)


def on_device(feats, requests, tile_dest, tile_slot, tile_vals, w_self, w_neigh, bias, cotangent):
    owners = lax.axis_size("blk")
    replicas = lax.axis_size("rep")
    blk_dev, tile_rows, features = feats.shape
    quarter = tile_rows // replicas
    per_owner = blk_dev // 2
    rep_index = lax.axis_index("rep")
    send_list = requests[0]
    slot_owner = tile_slot[0]
    ordering = jnp.argsort(slot_owner, stable=True)
    sorted_dest = jnp.take(tile_dest[0], ordering, axis=0)
    grouped = jnp.take(tile_vals[0], ordering, axis=0).reshape(
        owners, per_owner, quarter, tile_rows
    )
    dest_onehot = sorted_dest[:, None] == jnp.arange(blk_dev, dtype=jnp.int32)[None, :]
    own_rows = lax.dynamic_slice_in_dim(feats, rep_index * quarter, quarter, 1)
    outgoing = jnp.take(feats, send_list, axis=0)
    sources = lax.all_to_all(outgoing, "blk", split_axis=0, concat_axis=0, tiled=True)
    products = jnp.einsum("okij,ojd->okid", grouped, sources, preferred_element_type=jnp.float32)
    products = products.reshape(owners * per_owner, quarter * features)
    summed = jnp.dot(dest_onehot.astype(jnp.float32).T, products, precision=lax.Precision.HIGHEST)
    aggregate = summed.reshape(blk_dev, quarter, features).astype(jnp.bfloat16)
    row_count = blk_dev * quarter
    feat_rows = own_rows.reshape(row_count, features)
    agg_rows = aggregate.reshape(row_count, features)
    preact = jnp.dot(feat_rows, w_self, preferred_element_type=jnp.float32)
    preact = preact + jnp.dot(agg_rows, w_neigh, preferred_element_type=jnp.float32) + bias
    hidden = jax.nn.silu(preact).astype(jnp.bfloat16).reshape(blk_dev, quarter, features)
    gating = jax.nn.sigmoid(preact)
    grad_rows = cotangent.reshape(row_count, features).astype(jnp.float32)
    grad_pre = (grad_rows * gating * (1.0 + preact * (1.0 - gating))).astype(jnp.bfloat16)
    grad_scale = 1.0 / math.sqrt(owners * blk_dev * tile_rows)
    self_local = (
        jnp.einsum("nd,ne->de", feat_rows, grad_pre, preferred_element_type=jnp.float32)
        * grad_scale
    )
    neigh_local = (
        jnp.einsum("nd,ne->de", agg_rows, grad_pre, preferred_element_type=jnp.float32) * grad_scale
    )
    bias_local = jnp.sum(grad_pre.astype(jnp.float32), axis=0) * grad_scale
    grad_self, grad_neigh, grad_bias = lax.psum(
        (self_local, neigh_local, bias_local), ("rep", "blk")
    )
    back_rows = jnp.einsum(
        "ne,de->nd", grad_pre, w_neigh, preferred_element_type=jnp.float32
    ).astype(jnp.bfloat16)
    back_flat = back_rows.reshape(blk_dev, quarter * features)
    picked = jnp.dot(
        dest_onehot.astype(jnp.bfloat16), back_flat, preferred_element_type=jnp.float32
    ).astype(jnp.bfloat16)
    picked = picked.reshape(owners, per_owner, quarter, features)
    contributions = jnp.einsum(
        "okij,okid->ojd", grouped, picked, preferred_element_type=jnp.float32
    )
    self_term = jnp.einsum("ne,de->nd", grad_pre, w_self, preferred_element_type=jnp.float32)
    arrivals = lax.all_to_all(
        contributions.astype(jnp.bfloat16), "blk", split_axis=0, concat_axis=0, tiled=True
    ).astype(contributions.dtype)
    collected = collect_blocks(arrivals, send_list, blk_dev)
    neighbour = lax.psum_scatter(
        collected.astype(jnp.bfloat16), "rep", scatter_dimension=1, tiled=True
    ).astype(jnp.float32)
    feat_grad = (self_term.reshape(blk_dev, quarter, features) + neighbour).astype(jnp.bfloat16)
    return (hidden, grad_self, grad_neigh, grad_bias, feat_grad)


def solution(mesh):
    in_specs = (
        P("blk", None, None),
        P("blk", None),
        P("blk", None),
        P("blk", None),
        P("blk", None, "rep", None),
        P(),
        P(),
        P(),
        P("blk", "rep", None),
    )
    out_specs = (P("blk", "rep", None), P(), P(), P(), P("blk", "rep", None))
    return jax.shard_map(
        on_device, mesh=mesh, in_specs=in_specs, out_specs=out_specs, check_vma=False
    )
```

profile of v0, /device:TPU:2, one launch (start us, length us, event | category | flops | bytes accessed | tf_op | source)
XLA Modules:
  0.0 564.7 jit_solution(1460504856205556514)
XLA Ops:
  8.0 0.7 fusion.23
  8.8 0.7 compare_and_fusion
  9.4 2.8 gather_fusion.2
  12.2 4.6 broadcast_select_fusion
  16.8 12.3 %all-to-all-start = ((bf16[64,128,256]{2,1,0:T(8,128)(2,1)}), bf16[64,128,256]{2,1,0:T(8,128)(2,1)}, u32[]{:S(2)}, u32[]{:S(2)}) async-start(bf16[64,128,256]{2,1,0:T(8,128)(2,1)} %broadcast_select_fusion), calls=%async_computation | async-start | bytes 8388608 | tf_op jit(solution)/shard_map/all_to_all | solution.py:32
  29.3 3.8 sort.17
  33.0 3.5 gather_fusion
  36.6 0.1 broadcast_in_dim.36
  36.7 5.5 gather_fusion.1
  42.2 0.2 fusion.27
  42.4 81.6 %all-to-all-done = bf16[64,128,256]{2,1,0:T(8,128)(2,1)} async-done(((bf16[64,128,256]{2,1,0:T(8,128)(2,1)}), bf16[64,128,256]{2,1,0:T(8,128)(2,1)}, u32[]{:S(2)}, u32[]{:S(2)}) %all-to-all-start) | async-done | bytes 4194336 | tf_op jit(solution)/shard_map/all_to_all | solution.py:32
  124.0 4.9 convolution_bitcast_fusion
  128.9 17.9 %copy.29 = f32[64,8,32,256]{3,1,2,0:T(8,128)} copy(f32[64,8,32,256]{3,2,1,0:T(8,128)S(1)} %convolution_bitcast_fusion) | data formatting | bytes 33554432
  146.8 17.5 %copy.21 = f32[8192,512]{1,0:T(8,128)} copy(f32[8192,512]{0,1:T(8,128)} %bitcast.56) | data formatting | bytes 33554432 | tf_op jit(solution)/shard_map/dot_general | solution.py:35
  164.3 11.3 %convolution_convert_fusion.1 = bf16[16,32,256]{2,0,1:T(8,128)(2,1)S(1)} fusion(f32[32,256,512]{2,1,0:T(8,128)} %bitcast.55, s32[512]{0:T(512)S(1)} %get-tuple-element.26), kind=kOutput, calls=%fused_computation.18 | convolution fusion | flops 805445632 | bytes 17041408 | tf_op jit(solution)/shard_map/dot_general | solution.py:35
  175.6 0.1 copy.22
  175.7 1.1 convert_reduce_fusion
  176.9 0.3 convolution_convert_fusion.2
  177.1 0.1 reshape.89
  177.3 5.6 convolution_convert_fusion
  182.9 8.3 %bitcast_convert_fusion = bf16[64,128,256]{2,1,0:T(8,128)(2,1)} fusion(bf16[64,8,32,256]{3,1,2,0:T(8,128)(2,1)} %bitcast.59, bf16[64,8,32,128]{3,2,1,0:T(8,128)(2,1)S(1)} %bitcast.58, pred[64,8]{1,0:T(8,128)(4,1)S(1)} %broadcast_in_dim.36), kind=kOutput, calls=%fused_computation.5 | convolution fusion | flops 1077936128 | bytes 16777728 | tf_op jit(solution)/shard_map/okij,okid->ojd/dot_general | solution.py:66
  191.2 101.4 %all_to_all.10 = bf16[64,128,256]{2,1,0:T(8,128)(2,1)S(1)} all-to-all(bf16[64,128,256]{2,1,0:T(8,128)(2,1)} %bitcast_convert_fusion), channel_id=1, replica_groups=mesh['rep'=4,'blk'=64] {'blk'}, dimensions={0} | all-to-all | bytes 8388608 | tf_op jit(solution)/shard_map/all_to_all | solution.py:70
  292.6 3.3 fusion.9
  296.0 1.0 convolution_multiply_fusion
  297.0 1.0 convolution_multiply_fusion.1
  297.9 0.3 fusion.28
  298.2 76.7 %psum.23 = f32[256]{0:T(256)} all-reduce(f32[256]{0:T(256)S(1)} %broadcast_multiply_fusion), channel_id=1, replica_groups=mesh['rep'=4,'blk'=64] {'rep','blk'}, use_global_device_ids=true, to_apply=%region_4.5 | all-reduce | flops 256 | bytes 2048 | tf_op jit(solution)/shard_map/psum | solution.py:55
  374.9 1.2 fusion.15
  376.2 0.8 copy.26
  376.9 176.9 %all-reduce.3.cloned.1.call-done = (f32[256,256]{1,0:T(8,128)}, f32[256,256]{1,0:T(8,128)}) async-done(((f32[256,256]{1,0:T(8,128)}, f32[256,256]{1,0:T(8,128)}), (f32[256,256]{1,0:T(8,128)}, f32[256,256]{1,0:T(8,128)})) %all-reduce.3.cloned.1.call-update) | async-done | bytes 524304 | tf_op jit(solution)/shard_map/psum | solution.py:55
  553.9 1.7 copy.43
  555.6 1.7 copy.44
  (32 shorter events, 0.2 us)
Async XLA Ops:
  8.0 1.4 copy-start
  16.8 12.4 %copy-start.6 = (s32[1,512]{1,0:T(1,128)S(1)}, s32[1,512]{1,0:T(1,128)}, u32[]{:S(2)}) copy-start(s32[1,512]{1,0:T(1,128)} %param.12) | copy-start | bytes 6148
  16.8 16.2 %copy-start.2 = (s32[1,512]{1,0:T(1,128)S(1)}, s32[1,512]{1,0:T(1,128)}, u32[]{:S(2)}) copy-start(s32[1,512]{1,0:T(1,128)} %param.11) | copy-start | bytes 6148
  16.8 107.2 %all-to-all-start = ((bf16[64,128,256]{2,1,0:T(8,128)(2,1)}), bf16[64,128,256]{2,1,0:T(8,128)(2,1)}, u32[]{:S(2)}, u32[]{:S(2)}) async-start(bf16[64,128,256]{2,1,0:T(8,128)(2,1)} %broadcast_select_fusion), calls=%async_computation | async-start | bytes 8388608 | tf_op jit(solution)/shard_map/all_to_all | solution.py:32
  29.2 345.7 %reduce-scatter.2.cloned.1.call-start = ((), (), s32[]{:S(2)}) async-start(), calls=%async_computation.3 | async-start | bytes 1310720 | tf_op jit(solution)/shard_map/reduce_scatter | solution.py:74
  36.7 5.5 copy-start.4
  164.3 11.4 %copy-start.5 = (bf16[256,256]{1,0:T(8,128)(2,1)S(1)}, bf16[256,256]{1,0:T(8,128)(2,1)}, u32[]{:S(2)}) copy-start(bf16[256,256]{1,0:T(8,128)(2,1)} %param.15) | copy-start | bytes 393220
  164.3 11.4 %copy-start.8 = (bf16[16,32,256]{2,1,0:T(8,128)(2,1)S(1)}, bf16[16,32,256]{2,1,0:T(8,128)(2,1)}, u32[]{:S(2)}) copy-start(bf16[16,32,256]{2,1,0:T(8,128)(2,1)} %param.17) | copy-start | bytes 786436
  164.3 11.4 %copy-start.9 = (f32[256]{0:T(256)S(1)}, f32[256]{0:T(256)}, u32[]{:S(2)}) copy-start(f32[256]{0:T(256)} %param.16) | copy-start | bytes 3076
  177.3 5.6 copy-start.3
  191.2 101.4 %copy-start.7 = (s32[1,64]{1,0:T(1,128)S(1)}, s32[1,64]{1,0:T(1,128)}, u32[]{:S(2)}) copy-start(s32[1,64]{1,0:T(1,128)} %param.10) | copy-start | bytes 772
  292.6 264.6 %copy-start.1 = (bf16[16,128,256]{2,1,0:T(8,128)(2,1)S(1)}, bf16[16,128,256]{2,1,0:T(8,128)(2,1)}, u32[]{:S(2)}) copy-start(bf16[16,128,256]{2,1,0:T(8,128)(2,1)} %param.9) | copy-start | bytes 3145732
  295.9 257.9 %all-reduce.3.cloned.1.call-start = ((), (), s32[]{:S(2)}) async-start(), calls=%async_computation.4 | async-start | bytes 1048576 | tf_op jit(solution)/shard_map/psum | solution.py:55
Sparse Core Ops, SparseCore 0:
  296.1 24.7 reduce-scatter.1
Sparse Core Ops, SparseCore 1:
  302.6 251.2 all-reduce.2
where the time goes:
time: 565 us
  waiting for transfers between devices  259 us (46%)
  blocking collectives  178 us (32%)
  local copies, waits for them, and re-layouts  51.6 us (9%)
  matrix products  37.3 us (7%)
  between operations  15.7 us (3%)
  starting transfers between devices  12.4 us (2%)
  other arithmetic  11.1 us (2%)
    psum x1, waiting for transfers between devices, on_device(): lax.psum((self_local, neigh_local, bias_local), ('rep', 'blk'))  177 us
    all_to_all x1, blocking collectives, on_device(): lax.all_to_all(contributions.astype(jnp.bfloat16), 'blk', split_axis=0, c...  101 us
    all_to_all x1, waiting for transfers between devices, on_device(): lax.all_to_all(outgoing, 'blk', split_axis=0, concat_axis=0, tiled=True)  81.6 us
    psum x1, blocking collectives, on_device(): lax.psum((self_local, neigh_local, bias_local), ('rep', 'blk'))  76.7 us
    unnamed x24, local copies, waits for them, and re-layouts  22.1 us
    dot_general x1, local copies, waits for them, and re-layouts, on_device(): jnp.dot(dest_onehot.astype(jnp.float32).T, products, precision=lax.Precis...  17.5 us
    all_to_all x1, starting transfers between devices, on_device(): lax.all_to_all(outgoing, 'blk', split_axis=0, concat_axis=0, tiled=True)  12.3 us
    dot_general x1, matrix products, on_device(): jnp.dot(dest_onehot.astype(jnp.float32).T, products, precision=lax.Precis...  11.3 us
  transfers between devices with their start and end apart: 3, of which 2 were waited for; matrix products, arithmetic and copies ran while one was open for 3% of the time, Pallas kernels for 0%

commit v1 on v0

--- a/solution.py
+++ b/solution.py
@@ -3,6 +3,11 @@
 import jax.numpy as jnp
 from jax import lax
 from jax.sharding import PartitionSpec as P
+
+
+def store_body_on(mine):
+    reply = lax.psum(lax.psum(mine, "rep"), "blk")
+    return reply
 
 
 def collect_blocks(arrivals, send_list, blk_dev):
@@ -52,9 +57,7 @@
         jnp.einsum("nd,ne->de", agg_rows, grad_pre, preferred_element_type=jnp.float32) * grad_scale
     )
     bias_local = jnp.sum(grad_pre.astype(jnp.float32), axis=0) * grad_scale
-    grad_self, grad_neigh, grad_bias = lax.psum(
-        (self_local, neigh_local, bias_local), ("rep", "blk")
-    )
+    grad_self, grad_neigh, grad_bias = store_body_on((self_local, neigh_local, bias_local))
     back_rows = jnp.einsum(
         "ne,de->nd", grad_pre, w_neigh, preferred_element_type=jnp.float32
     ).astype(jnp.bfloat16)

time: 565 us -> 518 us (0.917)
  blocking collectives: 178 us -> 116 us
  starting transfers between devices: 12.4 us -> 19.5 us
  waiting for transfers between devices: 259 us -> 265 us
    all_to_all x1 -> x0, blocking collectives: 101 us -> none  [on_device(): lax.all_to_all(contributions.astype(jnp.bfloat16), 'blk', split_axis=0, c...]
    all_to_all x0 -> x1, waiting for transfers between devices: none -> 92.8 us  [on_device(): lax.all_to_all(contributions.astype(jnp.bfloat16), 'blk', split_axis=0, c...]
    psum x1 -> x2, waiting for transfers between devices: 177 us -> 90.4 us  [store_body_on(): reply = lax.psum(lax.psum(mine, 'rep'), 'blk')]
    psum x1 -> x2, blocking collectives: 76.7 us -> 116 us  [store_body_on(): reply = lax.psum(lax.psum(mine, 'rep'), 'blk')]
    all_to_all x0 -> x1, starting transfers between devices: none -> 7.08 us  [on_device(): lax.all_to_all(contributions.astype(jnp.bfloat16), 'blk', split_axis=0, c...]
  transfers between devices with their start and end apart: 3 -> 5, of which waited for: 2 -> 3; matrix products, arithmetic and copies ran while one was open for 3% -> 4% of each run, Pallas kernels for 0% -> 0%
where the time goes in v1:
time: 518 us; the launch traced here: 517 us
  waiting for transfers between devices  265 us (51%)
  blocking collectives  116 us (22%)
  local copies, waits for them, and re-layouts  51.6 us (10%)
  matrix products  39.5 us (8%)
  starting transfers between devices  19.5 us (4%)
  between operations  14 us (3%)
  other arithmetic  11 us (2%)
    psum x2, blocking collectives, store_body_on(): reply = lax.psum(lax.psum(mine, 'rep'), 'blk')  116 us
    all_to_all x1, waiting for transfers between devices, on_device(): lax.all_to_all(contributions.astype(jnp.bfloat16), 'blk', split_axis=0, c...  92.8 us
    psum x2, waiting for transfers between devices, store_body_on(): reply = lax.psum(lax.psum(mine, 'rep'), 'blk')  90.4 us
    all_to_all x1, waiting for transfers between devices, on_device(): lax.all_to_all(outgoing, 'blk', split_axis=0, concat_axis=0, tiled=True)  81.7 us
    unnamed x24, local copies, waits for them, and re-layouts  22.1 us
    dot_general x1, local copies, waits for them, and re-layouts, on_device(): jnp.dot(dest_onehot.astype(jnp.float32).T, products, precision=lax.Precis...  17.5 us
    all_to_all x1, starting transfers between devices, on_device(): lax.all_to_all(outgoing, 'blk', split_axis=0, concat_axis=0, tiled=True)  12.3 us
    dot_general x1, matrix products, on_device(): jnp.dot(dest_onehot.astype(jnp.float32).T, products, precision=lax.Precis...  11.3 us
  transfers between devices with their start and end apart: 5, of which 3 were waited for; matrix products, arithmetic and copies ran while one was open for 4% of the time, Pallas kernels for 0%

profile of v1, /device:TPU:2, one launch (start us, length us, event | category | flops | bytes accessed | tf_op | source)
XLA Modules:
  0.0 517.1 jit_solution(12777980673085022481)
XLA Ops:
  7.2 0.7 fusion.23
  7.9 0.7 compare_and_fusion
  8.6 2.8 gather_fusion.2
  11.4 4.6 broadcast_select_fusion
  16.0 12.3 %all-to-all-start = ((bf16[64,128,256]{2,1,0:T(8,128)(2,1)}), bf16[64,128,256]{2,1,0:T(8,128)(2,1)}, u32[]{:S(2)}, u32[]{:S(2)}) async-start(bf16[64,128,256]{2,1,0:T(8,128)(2,1)} %broadcast_select_fusion), calls=%async_computation | async-start | bytes 8388608 | tf_op jit(solution)/shard_map/all_to_all | solution.py:37
  28.4 3.8 sort.17
  32.2 3.5 gather_fusion
  35.8 5.5 %gather_fusion.1 = bf16[512,32,128]{2,1,0:T(8,128)(2,1)} fusion(bf16[512,32,128]{2,1,0:T(8,128)(2,1)} %bitcast.60, s32[1024]{0:T(1024)S(1)} %pad_clamp_fusion.1), kind=kCustom, calls=%fused_computation.1 | custom fusion | bytes 8390656 | tf_op jit(solution)/shard_map/jit(_take)/gather | solution.py:31
  41.3 0.2 fusion.27
  41.5 81.7 %all-to-all-done = bf16[64,128,256]{2,1,0:T(8,128)(2,1)} async-done(((bf16[64,128,256]{2,1,0:T(8,128)(2,1)}), bf16[64,128,256]{2,1,0:T(8,128)(2,1)}, u32[]{:S(2)}, u32[]{:S(2)}) %all-to-all-start) | async-done | bytes 4194336 | tf_op jit(solution)/shard_map/all_to_all | solution.py:37
  123.2 4.9 convolution_bitcast_fusion
  128.1 17.9 %copy.29 = f32[64,8,32,256]{3,1,2,0:T(8,128)} copy(f32[64,8,32,256]{3,2,1,0:T(8,128)S(1)} %convolution_bitcast_fusion) | data formatting | bytes 33554432
  146.0 17.5 %copy.21 = f32[8192,512]{1,0:T(8,128)} copy(f32[8192,512]{0,1:T(8,128)} %bitcast.56) | data formatting | bytes 33554432 | tf_op jit(solution)/shard_map/dot_general | solution.py:40
  163.4 11.3 %convolution_convert_fusion.1 = bf16[16,32,256]{2,0,1:T(8,128)(2,1)S(1)} fusion(f32[32,256,512]{2,1,0:T(8,128)} %bitcast.55, s32[512]{0:T(512)S(1)} %get-tuple-element.28), kind=kOutput, calls=%fused_computation.18 | convolution fusion | flops 805445632 | bytes 17041408 | tf_op jit(solution)/shard_map/dot_general | solution.py:40
  174.9 1.1 convert_reduce_fusion
  176.0 0.3 convolution_convert_fusion.2
  176.4 5.6 %convolution_convert_fusion = bf16[512,8192]{1,0:T(8,128)(2,1)} fusion(bf16[16,8192]{1,0:T(8,128)(2,1)S(1)} %reshape.89, s32[512]{0:T(512)S(1)} %get-tuple-element.28), kind=kOutput, calls=%fused_computation.3 | convolution fusion | flops 138420224 | bytes 8652800 | tf_op jit(solution)/shard_map/dot_general | solution.py:65
  182.0 8.3 %bitcast_convert_fusion = bf16[64,128,256]{2,1,0:T(8,128)(2,1)} fusion(bf16[64,8,32,256]{3,1,2,0:T(8,128)(2,1)} %bitcast.59, bf16[64,8,32,128]{3,2,1,0:T(8,128)(2,1)S(1)} %bitcast.58, pred[64,8]{1,0:T(8,128)(4,1)S(1)} %broadcast_in_dim.36), kind=kOutput, calls=%fused_computation.5 | convolution fusion | flops 1077936128 | bytes 16777728 | tf_op jit(solution)/shard_map/okij,okid->ojd/dot_general | solution.py:69
  190.4 7.1 %all-to-all-start.1 = ((bf16[64,128,256]{2,1,0:T(8,128)(2,1)}), bf16[64,128,256]{2,1,0:T(8,128)(2,1)}, u32[]{:S(2)}, u32[]{:S(2)}) async-start(bf16[64,128,256]{2,1,0:T(8,128)(2,1)} %bitcast_convert_fusion), calls=%async_computation.1 | async-start | bytes 8388608 | tf_op jit(solution)/shard_map/all_to_all | solution.py:73
  197.5 1.0 convolution_multiply_fusion
  198.5 1.0 convolution_multiply_fusion.1
  199.5 92.8 %all-to-all-done.1 = bf16[64,128,256]{2,1,0:T(8,128)(2,1)} async-done(((bf16[64,128,256]{2,1,0:T(8,128)(2,1)}), bf16[64,128,256]{2,1,0:T(8,128)(2,1)}, u32[]{:S(2)}, u32[]{:S(2)}) %all-to-all-start.1) | async-done | bytes 4194336 | tf_op jit(solution)/shard_map/all_to_all | solution.py:73
  292.3 5.6 %fusion.9 = bf16[16,128,256]{2,0,1:T(8,128)(2,1)} fusion(bf16[64,128,256]{2,1,0:T(8,128)(2,1)} %all-to-all-done.1, s32[64]{0:T(128)S(1)} %bitcast.67), kind=kOutput, calls=%fused_computation.15 | convolution fusion | flops 67634176 | bytes 5243136 | tf_op jit(solution)/shard_map/rb,rjd->bjd/dot_general | solution.py:17
  298.0 0.3 fusion.28
  298.3 0.4 all-reduce.5.cloned.1.call-update
  298.7 10.8 %psum.46 = f32[256]{0:T(256)S(1)} all-reduce(f32[256]{0:T(256)S(1)} %broadcast_multiply_fusion), channel_id=1, replica_groups=mesh['rep'=4,'blk'=64] {'rep'}, use_global_device_ids=true, to_apply=%region_6.7 | all-reduce | flops 256 | bytes 2048 | tf_op jit(solution)/shard_map/psum | solution.py:9
  309.5 105.3 %psum.47 = f32[256]{0:T(256)} all-reduce(f32[256]{0:T(256)S(1)} %psum.46), channel_id=1, replica_groups=mesh['rep'=4,'blk'=64] {'blk'}, use_global_device_ids=true, to_apply=%region_7.8 | all-reduce | flops 256 | bytes 2048 | tf_op jit(solution)/shard_map/psum | solution.py:9
  414.8 1.2 fusion.15
  416.0 0.8 copy.26
  416.8 90.4 %all-reduce.5.cloned.1.call-done = (f32[256,256]{1,0:T(8,128)}, f32[256,256]{1,0:T(8,128)}) async-done(((f32[256,256]{1,0:T(8,128)}, f32[256,256]{1,0:T(8,128)}), (f32[256,256]{1,0:T(8,128)}, f32[256,256]{1,0:T(8,128)})) %all-reduce.5.cloned.1.call-update) | async-done | bytes 524304 | tf_op jit(solution)/shard_map/psum | solution.py:9
  507.2 1.7 copy.45
  508.9 1.7 copy.46
  (37 shorter events, 0.6 us)
Async XLA Ops:
  7.2 1.4 copy-start
  16.0 12.4 %copy-start.6 = (s32[1,512]{1,0:T(1,128)S(1)}, s32[1,512]{1,0:T(1,128)}, u32[]{:S(2)}) copy-start(s32[1,512]{1,0:T(1,128)} %param.12) | copy-start | bytes 6148
  16.0 16.2 %copy-start.2 = (s32[1,512]{1,0:T(1,128)S(1)}, s32[1,512]{1,0:T(1,128)}, u32[]{:S(2)}) copy-start(s32[1,512]{1,0:T(1,128)} %param.11) | copy-start | bytes 6148
  16.0 107.2 %all-to-all-start = ((bf16[64,128,256]{2,1,0:T(8,128)(2,1)}), bf16[64,128,256]{2,1,0:T(8,128)(2,1)}, u32[]{:S(2)}, u32[]{:S(2)}) async-start(bf16[64,128,256]{2,1,0:T(8,128)(2,1)} %broadcast_select_fusion), calls=%async_computation | async-start | bytes 8388608 | tf_op jit(solution)/shard_map/all_to_all | solution.py:37
  35.8 5.5 %copy-start.4 = (bf16[256,256]{1,0:T(8,128)(2,1)S(1)}, bf16[256,256]{1,0:T(8,128)(2,1)}, u32[]{:S(2)}) copy-start(bf16[256,256]{1,0:T(8,128)(2,1)} %param.14) | copy-start | bytes 393220
  163.4 11.4 %copy-start.5 = (bf16[256,256]{1,0:T(8,128)(2,1)S(1)}, bf16[256,256]{1,0:T(8,128)(2,1)}, u32[]{:S(2)}) copy-start(bf16[256,256]{1,0:T(8,128)(2,1)} %param.15) | copy-start | bytes 393220
  163.4 11.4 %copy-start.8 = (bf16[16,32,256]{2,1,0:T(8,128)(2,1)S(1)}, bf16[16,32,256]{2,1,0:T(8,128)(2,1)}, u32[]{:S(2)}) copy-start(bf16[16,32,256]{2,1,0:T(8,128)(2,1)} %param.17) | copy-start | bytes 786436
  163.4 11.4 %copy-start.9 = (f32[256]{0:T(256)S(1)}, f32[256]{0:T(256)}, u32[]{:S(2)}) copy-start(f32[256]{0:T(256)} %param.16) | copy-start | bytes 3076
  176.4 5.6 %copy-start.3 = (bf16[512,32,128]{2,1,0:T(8,128)(2,1)S(1)}, bf16[512,32,128]{2,1,0:T(8,128)(2,1)}, u32[]{:S(2)}) copy-start(bf16[512,32,128]{2,1,0:T(8,128)(2,1)} %gather_fusion.1) | copy-start | bytes 12582916
  190.4 102.0 %copy-start.7 = (s32[1,64]{1,0:T(1,128)S(1)}, s32[1,64]{1,0:T(1,128)}, u32[]{:S(2)}) copy-start(s32[1,64]{1,0:T(1,128)} %param.10) | copy-start | bytes 772
  190.4 101.9 %all-to-all-start.1 = ((bf16[64,128,256]{2,1,0:T(8,128)(2,1)}), bf16[64,128,256]{2,1,0:T(8,128)(2,1)}, u32[]{:S(2)}, u32[]{:S(2)}) async-start(bf16[64,128,256]{2,1,0:T(8,128)(2,1)} %bitcast_convert_fusion), calls=%async_computation.1 | async-start | bytes 8388608 | tf_op jit(solution)/shard_map/all_to_all | solution.py:73
  197.5 100.8 %all-reduce.7.cloned.1.call-start = ((), (), s32[]{:S(2)}) async-start(), calls=%async_computation.5 | async-start | bytes 1048576 | tf_op jit(solution)/shard_map/psum | solution.py:9
  199.5 215.3 %reduce-scatter.2.cloned.1.call-start = ((), (), s32[]{:S(2)}) async-start(), calls=%async_computation.3 | async-start | bytes 1310720 | tf_op jit(solution)/shard_map/reduce_scatter | solution.py:77
  292.3 218.3 %copy-start.1 = (bf16[16,128,256]{2,1,0:T(8,128)(2,1)S(1)}, bf16[16,128,256]{2,1,0:T(8,128)(2,1)}, u32[]{:S(2)}) copy-start(bf16[16,128,256]{2,1,0:T(8,128)(2,1)} %param.9) | copy-start | bytes 3145732
  298.0 209.3 %all-reduce.5.cloned.1.call-start = ((), (), s32[]{:S(2)}) async-start(), calls=%async_computation.4 | async-start | bytes 1048576 | tf_op jit(solution)/shard_map/psum | solution.py:9
Sparse Core Ops, SparseCore 0:
  201.3 49.4 all-reduce.6
  298.1 23.8 reduce-scatter.1
  326.0 181.2 all-reduce.4
